TPU v7x, 256 devices: a whole 4x4x8 slice. The times are simulated.
256 devices in a mesh: frame: 64 (over y, z, x_lo), band: 4 (over x_hi, core).
Axes of the slice: x: 4 (x_hi: 2, x_lo: 2; x = x_hi * 2 + x_lo), y: 4, z: 8, core: 2. Of those that a mesh axis runs over, the one named last changes fastest.
Arguments:
- latents: bfloat16 [64, 64, 32, 640], P('frame', 'band'), may hold values from -90 to 90, as said below
- conv_weight: bfloat16 [3, 3, 640, 640], replicated, may hold values from -0.078125 to 0.078125
- conv_bias: bfloat16 [640], replicated, may hold values from -3 to 3
- w_query: bfloat16 [640, 640], replicated, may hold values from -0.25 to 0.25
- w_keyval: bfloat16 [640, 1280], replicated, may hold values from -0.25 to 0.25
- w_out: bfloat16 [640, 640], replicated, may hold values from -0.25 to 0.25
Outputs:
- result: bfloat16 [64, 64, 32, 640], P('frame', 'band')
Inputs may be any that keep to these rules, and one draw needn't show every extreme that they name: `latents`: latent features; some frames may be far larger in magnitude than others.
All inputs are finite; a program needn't handle non-finite values.
Results may differ from a plain program's by a relative error of at most 0.023.
Values may be sent and summed in bfloat16 or wider, within the bound.
A program may use at most 128 MiB of HBM per device.

v0:
```python
import jax
import jax.numpy as jnp
from jax import lax
from jax.sharding import PartitionSpec as P

HEAD_DIM = 64


key_block = 512


def with_halo(block, sides, width):
    for axis, dim in sides:
        count = lax.axis_size(axis)
        forward = [(i, i + 1) for i in range(count - 1)]
        backward = [(target, source) for source, target in forward]
        low = lax.ppermute(
            lax.slice_in_dim(block, block.shape[dim] - width, None, axis=dim), axis, forward
        )
        high = lax.ppermute(lax.slice_in_dim(block, 0, width, axis=dim), axis, backward)
        block = jnp.concatenate([low, block, high], axis=dim)
    return block


def spread(value, axis, source):
    kept = jnp.where(lax.axis_index(axis) == source, value, 0).astype(value.dtype)
    return lax.psum(kept, axis)


def absorb_block(running, queries, keyval, channels):
    row_best, weight_sum, weighted = running
    head_count = channels // HEAD_DIM
    query_count = queries.shape[0]
    key_count = keyval.shape[0]
    query_heads = queries.reshape(query_count, head_count, HEAD_DIM)
    key_heads = keyval[:, :channels].reshape(key_count, head_count, HEAD_DIM)
    value_heads = keyval[:, channels:].reshape(key_count, head_count, HEAD_DIM)
    scores = jnp.einsum(
        "qhd,khd->hqk", query_heads, key_heads, preferred_element_type=jnp.float32
    ) * HEAD_DIM ** (-0.5)
    new_best = jnp.maximum(row_best, jnp.max(scores, axis=2))
    fading = jnp.exp(row_best - new_best)
    probability = jnp.exp(scores - new_best[:, :, None])
    weight_sum = weight_sum * fading + jnp.sum(probability, axis=2)
    update = jnp.einsum(
        "hqk,khd->qhd",
        probability.astype(jnp.bfloat16),
        value_heads,
        preferred_element_type=jnp.float32,
    )
    weighted = weighted * jnp.transpose(fading)[:, :, None] + update
    return (new_best, weight_sum, weighted)


def fold_keys(running, queries, keyval, channels):
    key_count = keyval.shape[0]
    block_rows = min(key_count, key_block)

    def advance(position, partial_value):
        rows_now = lax.dynamic_slice_in_dim(keyval, position * block_rows, block_rows, 0)
        return absorb_block(partial_value, queries, rows_now, channels)

    return lax.fori_loop(0, key_count // block_rows, advance, running)


def per_device(latents, conv_weight, conv_bias, w_query, w_keyval, w_out):
    frames, row_count, col_count, channels = latents.shape
    tokens = frames * row_count * col_count
    activated = jax.nn.silu(latents.astype(jnp.float32)).astype(jnp.bfloat16)
    rimmed = with_halo(activated, (("band", 1),), 1)
    padded = jnp.pad(rimmed, ((0, 0), (0, 0), (1, 1), (0, 0)))
    summed = jnp.zeros((tokens, channels), jnp.float32)
    for row_shift in range(3):
        for col_shift in range(3):
            window = padded[
                :, row_shift : row_shift + row_count, col_shift : col_shift + col_count
            ].reshape(tokens, channels)
            summed = summed + jnp.dot(
                window, conv_weight[row_shift, col_shift], preferred_element_type=jnp.float32
            )
    hidden = (
        latents.reshape(tokens, channels).astype(jnp.float32)
        + summed
        + conv_bias.astype(jnp.float32)
    ).astype(jnp.bfloat16)
    queries = jnp.dot(hidden, w_query, preferred_element_type=jnp.float32).astype(jnp.bfloat16)
    payload = jnp.dot(hidden, w_keyval, preferred_element_type=jnp.float32).astype(jnp.bfloat16)
    head_count = channels // HEAD_DIM
    start_state = (
        jnp.full((head_count, tokens), -jnp.inf, jnp.float32),
        jnp.zeros((head_count, tokens), jnp.float32),
        jnp.zeros((tokens, head_count, HEAD_DIM), jnp.float32),
    )
    joined = lax.all_gather(payload, "band", axis=0, tiled=True)
    joined = spread(joined, "frame", 0)
    row_best, weight_sum, weighted = fold_keys(start_state, queries, joined, channels)
    mixed = (
        (weighted / jnp.transpose(weight_sum)[:, :, None])
        .reshape(tokens, channels)
        .astype(jnp.bfloat16)
    )
    output = hidden.astype(jnp.float32) + jnp.dot(mixed, w_out, preferred_element_type=jnp.float32)
    return output.astype(jnp.bfloat16).reshape(frames, row_count, col_count, channels)


def solution(mesh):
    return jax.shard_map(
        per_device,
        mesh=mesh,
        in_specs=(P("frame", "band", None, None), P(), P(), P(), P(), P()),
        out_specs=P("frame", "band", None, None),
        check_vma=False,
    )
```

profile of v0, /device:TPU:4, one launch (start us, length us, event | category | flops | bytes accessed | tf_op | source)
XLA Modules:
  0.0 796.2 jit_solution(4253323085686265464)
XLA Ops:
  8.2 1.9 collective-permute-start
  10.1 5.1 collective-permute-start.1
  17.7 2.6 copy-done.2
  27.7 2.3 convolution_convert_fusion
  30.2 47.6 %all-gather.2.cloned.1.call-done = bf16[2048,1280]{1,0:T(8,128)(2,1)} async-done(((bf16[512,1280]{1,0:T(8,128)(2,1)}), bf16[2048,1280]{1,0:T(8,128)(2,1)}) %all-gather.2.cloned.1.call-update) | async-done | bytes 5242896 | tf_op jit(solution)/shard_map/all_gather | solution.py:94
  77.8 5.1 broadcast_select_fusion
  83.0 1.9 convolution_convert_fusion.1
  86.0 621.0 %all-reduce.3.cloned.1.call-done = bf16[2048,1280]{1,0:T(8,128)(2,1)} async-done(((bf16[2048,1280]{1,0:T(8,128)(2,1)}), bf16[2048,1280]{1,0:T(8,128)(2,1)}) %all-reduce.3.cloned.1.call-update) | async-done | bytes 5242896 | tf_op jit(solution)/shard_map/psum | solution.py:27
  707.0 79.0 %while.18 = (s32[]{:T(128)}, f32[10,512]{1,0:T(8,128)S(1)}, f32[10,512]{1,0:T(8,128)S(1)}, f32[512,10,64]{0,2,1:T(8,128)}, bf16[2048,1280]{1,0:T(8,128)(2,1)}, /...) while((s32[]{:T(128)}, f32[10,512]{1,0:T(8,128)S(1)}, ...), condition=%wide.region_4.5_spmd.clone, body=%wide.region_1.4_spmd.clone.sunk | while | flops 693073920 | bytes 83558608 | solution.py:63
  707.0 2.2 fusion.81
  710.5 6.6 bitcast_reduce_fusion.2
  717.5 7.2 fusion.85
  724.7 1.7 fusion.83
  726.5 2.3 fusion.81
  730.1 6.6 bitcast_reduce_fusion.2
  737.0 7.5 fusion.85
  744.5 1.7 fusion.83
  746.3 2.3 fusion.81
  749.9 6.6 bitcast_reduce_fusion.2
  756.9 7.5 fusion.85
  764.4 1.7 fusion.83
  766.2 2.3 fusion.81
  769.8 6.6 bitcast_reduce_fusion.2
  776.7 7.5 fusion.85
  (69 shorter events, 24.2 us)
Async XLA Ops:
  6.5 21.1 %copy-start = (bf16[640,1280]{1,0:T(8,128)(2,1)S(1)}, bf16[640,1280]{1,0:T(8,128)(2,1)}, u32[]{:S(2)}) copy-start(bf16[640,1280]{1,0:T(8,128)(2,1)} %param.12) | copy-start | bytes 4915204
  6.5 8.7 %copy-start.6 = (bf16[640]{0:T(1024)(128)(2,1)S(1)}, bf16[640]{0:T(1024)(128)(2,1)}, u32[]{:S(2)}) copy-start(bf16[640]{0:T(1024)(128)(2,1)} %param.10) | copy-start | bytes 3844
  6.5 71.2 %all-gather.2.cloned.1.call-start = ((), (), s32[]{:S(2)}) async-start(), calls=%async_computation | async-start | bytes 6553600 | tf_op jit(solution)/shard_map/all_gather | solution.py:94
  8.2 7.1 collective-permute-start
  10.1 6.8 collective-permute-start.1
  17.2 3.1 copy-start.2
  25.8 1.1 copy-start.3
  27.7 55.3 %copy-start.4 = (bf16[512,640]{1,0:T(8,128)(2,1)}, bf16[512,640]{1,0:T(8,128)(2,1)S(1)}, u32[]{:S(2)}) copy-start(bf16[512,640]{1,0:T(8,128)(2,1)S(1)} %fusion.20) | copy-start | bytes 1966084
  30.0 677.0 %all-reduce.3.cloned.1.call-start = ((), (), s32[]{:S(2)}) async-start(), calls=%async_computation.1 | async-start | bytes 10485760 | tf_op jit(solution)/shard_map/psum | solution.py:27
  717.5 7.2 copy-start.1
  737.0 7.5 copy-start.1
  756.8 7.5 copy-start.1
  776.7 7.5 copy-start.1
  786.0 1.6 copy-start.5
  786.0 1.7 copy-start.7
Sparse Core Ops, SparseCore 0:
  30.1 47.6 all-gather.1
  83.0 623.8 all-reduce.2
where the time goes:
time: 797 us; the launch traced here: 796 us
  waiting for transfers between devices  670 us (84%)
  matrix products  69 us (9%)
  local copies, waits for them, and re-layouts  20 us (3%)
  other arithmetic  15.8 us (2%)
  between operations  13.7 us (2%)
    psum x1, waiting for transfers between devices, spread(): return lax.psum(kept, axis)  621 us
    all_gather x1, waiting for transfers between devices, per_device(): joined = lax.all_gather(payload, 'band', axis=0, tiled=True)  47.6 us
    dot_general x4, matrix products, absorb_block(): jnp.einsum('hqk,khd->qhd', probability.astype(jnp.bfloat16), value_heads,...  29.8 us
    dot_general x4, matrix products, absorb_block(): jnp.einsum('qhd,khd->hqk', query_heads, key_heads, preferred_element_type...  26.6 us
  transfers between devices with their start and end apart: 4, of which 3 were waited for; matrix products, arithmetic and copies ran while one was open for 0% of the time, Pallas kernels for 0%

commit v1 on v0

v1 whole, which is shorter than its diff:
```python
import jax
import jax.numpy as jnp
from jax import lax
from jax.experimental import pallas as pl
from jax.experimental.pallas import tpu as pltpu
from jax.sharding import PartitionSpec as P

BF = jnp.bfloat16
F32 = jnp.float32
MESH = pl.DeviceIdType.MESH
ROWS, COLS, C = 16, 32, 640
TOK = ROWS * COLS
KEYS = 4 * TOK
CH = 32
NCH = TOK // CH
LAG = 8
SCALE = 0.125 * 1.4426950408889634

TABLE = (
    (
        (1436916138, -2057218667, -1442141558, -1470609788, 0, 0, 5376, 268435456),
        (1788127785, 627464597, 0, 0, 0, 0, 1434801189, 1436913753),
        (-1434081239, 4456464, -1610046968, 1146093568, 18874400, 5242880, 562473, 2048),
        (1074833577, 1076363344, 336392, 167772176, 512, 671088656, 37513, -1539309568),
        (-2139029462, 8454224, 0, 360472, 0, -2147450880, 4129, 8),
        (1409394690, 67702792, 537395200, 1611202560, 1024, 0, 529736, 4261896),
        (524288, 262145, 0, 0, 0, 0, 0, 0),
        (0, 1073741825, 67117058, 134217728, 67108864, 0, 67108865, 0),
    ),
    (
        (0, 0, 2097184, 131104, -1705399670, 1686720645, 1435861144, 1113957700),
        (0, 0, -1469437406, -1717937510, -1441158566, -1722216432, 0, 0),
        (2097664, 1342252032, 178323586, 268780544, 1753918089, 1074004992, -1974337408, 1342472192),
        (88342528, 65536, 1073741986, -2142632960, 357607593, -2112815104, 89196576, 2629632),
        (0, 0, 5243232, 134217729, 5243010, 9437249, -2146893816, 9764864),
        (0, 0, 1074855936, 1086465, 1343856642, 1074860032, 65536, 1074302976),
        (0, 0, 131074, 2097152, 65544, 65540, 1048576, 16),
        (0, 0, 0, 0, 0, 268435457, 1073741824, 268435456),
    ),
)

STEPS = ((1, 0, 0), (-1, 0, 0), (0, 1, 0), (0, -1, 0), (0, 0, 1), (0, 0, -1), (0, 0, 2), (0, 0, -2))


def lookup(words, word, bit):
    value = jnp.int32(words[0])
    for k in range(1, 8):
        value = jnp.where(word == k, jnp.int32(words[k]), value)
    return lax.shift_right_logical(value, bit) & 1


def silu(v):
    v = v.astype(F32)
    return v * jax.nn.sigmoid(v)


def place(pad, act, row0):
    n = act.shape[0]
    col = lax.broadcasted_iota(jnp.int32, (n, 1), 0) % COLS
    pad[1, row0 : row0 + n] = act.astype(BF)
    pad[0, row0 : row0 + n] = jnp.where(col == 0, 0.0, pltpu.roll(act, 1, 0)).astype(BF)
    pad[2, row0 : row0 + n] = jnp.where(col == COLS - 1, 0.0, pltpu.roll(act, n - 1, 0)).astype(BF)


def spread_kernel(
    x_ref, w_hbm, b_ref, wq_ref, hid_ref, q_ref, h0_ref,
    wbuf, pad, halo, acc, wsem, hsend, hrecv, recv, send,
):
    f = lax.axis_index("frame")
    b = lax.axis_index("band")
    core = b % 2
    x = (b // 2) * 2 + f % 2
    y = f // 16
    z = (f // 2) % 8

    def chip(step):
        nx, ny, nz = (x + step[0] + 4) % 4, (y + step[1] + 4) % 4, (z + step[2] + 8) % 8
        return (ny * 16 + nz * 2 + nx % 2, (nx // 2) * 2 + core)

    targets = [chip(step) for step in STEPS]
    partner = (f, b + 1 - 2 * core)

    weights = [pltpu.make_async_copy(w_hbm.at[i], wbuf.at[i], wsem.at[i]) for i in range(3)]
    for i in (1, 0, 2):
        weights[i].start()

    barrier = pltpu.get_barrier_semaphore()
    for target in targets + [partner]:
        pl.semaphore_signal(barrier, inc=1, device_id=target, device_id_type=MESH)
    middle = (b == 1) | (b == 2)

    @pl.when(middle)
    def _():
        pl.semaphore_signal(barrier, inc=1, device_id=(f, 3 - b), device_id_type=MESH)

    pl.semaphore_wait(barrier, jnp.where(middle, 10, 9))

    def halo_copy(rows, slot, target):
        return pltpu.make_async_remote_copy(
            src_ref=x_ref.at[pl.ds(rows, COLS)], dst_ref=halo.at[slot],
            send_sem=hsend.at[slot], recv_sem=hrecv.at[slot],
            device_id=target, device_id_type=MESH,
        )

    up = halo_copy(0, 1, (f, jnp.maximum(b - 1, 0)))
    down = halo_copy(TOK - COLS, 0, (f, jnp.minimum(b + 1, 3)))

    @pl.when(b > 0)
    def _():
        up.start()

    @pl.when(b < 3)
    def _():
        down.start()

    place(pad, silu(x_ref[...]), COLS)
    acc[...] = x_ref[...].astype(F32) + b_ref[...].astype(F32)

    def tap(i):
        weights[i].wait()
        window = jnp.concatenate([pad[c, i * COLS : i * COLS + TOK] for c in range(3)], axis=1)
        acc[...] += jnp.dot(window, wbuf[i], preferred_element_type=F32)

    tap(1)

    @pl.when(b > 0)
    def _():
        up.wait_send()
        down.wait_recv()
        place(pad, silu(halo[0]), 0)

    @pl.when(b == 0)
    def _():
        pad[:, 0:COLS] = jnp.zeros((3, COLS, C), BF)

    @pl.when(b < 3)
    def _():
        down.wait_send()
        up.wait_recv()
        place(pad, silu(halo[1]), TOK + COLS)

    @pl.when(b == 3)
    def _():
        pad[:, TOK + COLS :] = jnp.zeros((3, COLS, C), BF)

    tap(0)
    tap(2)
    hidden = acc[...].astype(BF)
    hid_ref[...] = hidden

    @pl.when(f == 0)
    def _():
        h0_ref[pl.ds(pl.multiple_of(b * TOK, TOK), TOK), :] = hidden

    q_ref[...] = (jnp.dot(hidden, wq_ref[...], preferred_element_type=F32) * SCALE).astype(BF)

    index = ((x * 4 + y) * 8 + z) * 2 + core
    flags = [[lookup(TABLE[g][a], index // 32, index % 32) for a in range(8)] for g in range(2)]
    lags = [jnp.where(x == 2, LAG, 0), jnp.where(x == 0, LAG, 0)]

    def piece(band, k, g, arc, target):
        rows = h0_ref.at[pl.ds(pl.multiple_of(band * TOK + k * CH, CH), CH)]
        return pltpu.make_async_remote_copy(
            src_ref=rows, dst_ref=rows, send_sem=send.at[g, k, arc], recv_sem=recv.at[band, k],
            device_id=target, device_id_type=MESH,
        )

    def slot(s, _):
        for g in range(2):
            band = core + 2 * g
            k = s - lags[g]

            @pl.when((k >= 0) & (k < NCH))
            def _():
                @pl.when((f != 0) | (b != band))
                def _():
                    piece(band, k, g, 8, partner).wait_recv()

                for a in range(8):
                    @pl.when(flags[g][a] == 1)
                    def _():
                        piece(band, k, g, a, targets[a]).start()

                piece(band, k, g, 8, partner).start()

        return 0

    lax.fori_loop(0, NCH + LAG, slot, 0)

    def finish(k, _):
        for g in range(2):
            band = core + 2 * g
            for a in range(8):
                @pl.when(flags[g][a] == 1)
                def _():
                    piece(band, k, g, a, targets[a]).wait_send()

            piece(band, k, g, 8, partner).wait_send()
            piece(1 - core + 2 * g, k, g, 8, partner).wait_recv()
        return 0

    lax.fori_loop(0, NCH, finish, 0)


def attend_kernel(h_ref, q_ref, h0_ref, wkv_ref, wout_ref, o_ref, keys, values, mix):
    lane = lax.broadcasted_iota(jnp.int32, (1, 128), 1)
    values[:, 128:] = jnp.ones((KEYS, 128), BF)
    block = 128

    @pl.loop(0, 5)
    def _(j):
        c = pl.multiple_of(j * 128, 128)
        w = jnp.concatenate([wkv_ref[:, pl.ds(c, 128)], wkv_ref[:, pl.ds(pl.multiple_of(C + c, 128), 128)]], axis=1)
        kv = jnp.dot(h0_ref[...], w, preferred_element_type=F32).astype(BF)
        keys[...] = kv[:, :128]
        values[:, :128] = kv[:, 128:]
        for half in range(2):
            keep = (lane < 64) if half == 0 else (lane >= 64)
            for r in range(TOK // block):
                rows = slice(r * block, (r + 1) * block)
                head = jnp.where(keep, q_ref[rows, pl.ds(c, 128)], jnp.zeros((), BF))
                scores = lax.dot_general(head, keys[...], (((1,), (1,)), ((), ())), preferred_element_type=F32)
                best = jnp.max(scores, axis=1, keepdims=True)
                prob = jnp.exp2(scores - best).astype(BF)
                out = jnp.dot(prob, values[...], preferred_element_type=F32)
                out = (out[:, :128] / out[:, 128:]).astype(BF)
                if half == 1:
                    out = jnp.where(keep, out, mix[rows, pl.ds(c, 128)])
                mix[rows, pl.ds(c, 128)] = out

    o_ref[...] = (
        h_ref[...].astype(F32) + jnp.dot(mix[...], wout_ref[...], preferred_element_type=F32)
    ).astype(BF)


def per_device(latents, conv_weight, conv_bias, w_query, w_keyval, w_out):
    vmem = pl.BlockSpec(memory_space=pltpu.VMEM)
    tokens = jax.ShapeDtypeStruct((TOK, C), BF)
    hidden, queries, first = pl.pallas_call(
        spread_kernel,
        out_shape=[tokens, tokens, jax.ShapeDtypeStruct((KEYS, C), BF)],
        in_specs=[vmem, pl.BlockSpec(memory_space=pl.ANY), vmem, vmem],
        out_specs=[vmem, vmem, vmem],
        scratch_shapes=[
            pltpu.VMEM((3, 3 * C, C), BF),
            pltpu.VMEM((3, TOK + 2 * COLS, C), BF),
            pltpu.VMEM((2, COLS, C), BF),
            pltpu.VMEM((TOK, C), F32),
            pltpu.SemaphoreType.DMA((3,)),
            pltpu.SemaphoreType.DMA((2,)),
            pltpu.SemaphoreType.DMA((2,)),
            pltpu.SemaphoreType.DMA((4, NCH)),
            pltpu.SemaphoreType.DMA((2, NCH, 9)),
        ],
        compiler_params=pltpu.CompilerParams(collective_id=0, has_side_effects=True),
        name="spread",
    )(latents.reshape(TOK, C), conv_weight.reshape(3, 3 * C, C), conv_bias.reshape(1, C), w_query)
    result = pl.pallas_call(
        attend_kernel,
        out_shape=tokens,
        in_specs=[vmem] * 5,
        out_specs=vmem,
        scratch_shapes=[
            pltpu.VMEM((KEYS, 128), BF),
            pltpu.VMEM((KEYS, 256), BF),
            pltpu.VMEM((TOK, C), BF),
        ],
        name="attend",
    )(hidden, queries, first, w_keyval, w_out)
    return result.reshape(latents.shape)


def solution(mesh):
    return jax.shard_map(
        per_device,
        mesh=mesh,
        in_specs=(P("frame", "band", None, None), P(), P(), P(), P(), P()),
        out_specs=P("frame", "band", None, None),
        check_vma=False,
    )
```

time: 797 us -> 189 us (0.24)
  the two profiles are of different devices: /device:TPU:4 before, /device:TPU:65 now
where the time goes in v1:
time: 189 us
  Pallas kernels  188 us (99%)
    pallas_call x1, Pallas kernels, per_device(): pl.pallas_call(spread_kernel, out_shape=[tokens, tokens, jax.ShapeDtypeSt...  156 us
    pallas_call x1, Pallas kernels, per_device(): pl.pallas_call(attend_kernel, out_shape=tokens, in_specs=[vmem] * 5, out_...  32.3 us

profile of v1, /device:TPU:65, one launch (start us, length us, event | category | flops | bytes accessed | tf_op | source)
XLA Modules:
  0.0 189.2 jit_solution(4373286375895477047)
XLA Ops:
  0.0 1.3 reshape.14.b_ref
  1.3 155.6 %spread.1 = (bf16[512,640]{1,0:T(8,128)(2,1)}, bf16[512,640]{1,0:T(8,128)(2,1)}, bf16[2048,640]{1,0:T(8,128)(2,1)}) custom-call(bf16[512,640]{1,0:T(8,128)(2,1)} %bitcast.4, bf16[3,1920,640]{2,1,0:T(8,128)(2,1)} %bitcast.3, bf16[1,640]{1,0:T(2,128)(2,1)} %reshape.14.b_ref, bf16[640,640]{1,0:T(8,128)(2,1)} %wq_ref.1), custom_call_target="tpu_custom_call" | custom-call | tf_op jit(solution)/shard_map/spread/pallas_call | solution.py:239
  156.8 32.3 %attend.1 = bf16[512,640]{1,0:T(8,128)(2,1)} custom-call(bf16[512,640]{1,0:T(8,128)(2,1)} %get-tuple-element.8.h_ref, bf16[512,640]{1,0:T(8,128)(2,1)} %get-tuple-element.9.q_ref, bf16[2048,640]{1,0:T(8,128)(2,1)} %get-tuple-element.10.h0_ref, bf16[640,1280]{1,0:T(8,128)(2,1)} %wkv_ref.1, bf16[640,640]{1,0:T(8,128)(2,1)} %wout_ref.1), custom_call_target="tpu_custom_call" | custom-call | tf_op jit(solution)/shard_map/attend/pallas_call | solution.py:258

commit v2 on v1

--- a/solution.py
+++ b/solution.py
@@ -11,40 +11,68 @@
 ROWS, COLS, C = 16, 32, 640
 TOK = ROWS * COLS
 KEYS = 4 * TOK
-CH = 32
-NCH = TOK // CH
-LAG = 8
+NCH = 8
+PART = TOK // 2
+CH = PART // NCH
 SCALE = 0.125 * 1.4426950408889634
 
-TABLE = (
+ARCS = (
     (
-        (1436916138, -2057218667, -1442141558, -1470609788, 0, 0, 5376, 268435456),
-        (1788127785, 627464597, 0, 0, 0, 0, 1434801189, 1436913753),
-        (-1434081239, 4456464, -1610046968, 1146093568, 18874400, 5242880, 562473, 2048),
-        (1074833577, 1076363344, 336392, 167772176, 512, 671088656, 37513, -1539309568),
-        (-2139029462, 8454224, 0, 360472, 0, -2147450880, 4129, 8),
-        (1409394690, 67702792, 537395200, 1611202560, 1024, 0, 529736, 4261896),
-        (524288, 262145, 0, 0, 0, 0, 0, 0),
-        (0, 1073741825, 67117058, 134217728, 67108864, 0, 67108865, 0),
+        (157049088, -1860284160, 0, 4),
+        (92823553, 0, 2, 1860249119),
+        (-2011160575, -1946156796, -2147483648, -2147454715),
+        (-1929092543, 160064, 24576, 67133456),
+        (201408768, 402718720, 16384, 83969292),
+        (83914784, 88150272, 0, -2130706428),
+        (16777216, 16777216, 0, 134217729),
+        (4260096, 16384, 8192, 16384),
     ),
     (
-        (0, 0, 2097184, 131104, -1705399670, 1686720645, 1435861144, 1113957700),
-        (0, 0, -1469437406, -1717937510, -1441158566, -1722216432, 0, 0),
-        (2097664, 1342252032, 178323586, 268780544, 1753918089, 1074004992, -1974337408, 1342472192),
-        (88342528, 65536, 1073741986, -2142632960, 357607593, -2112815104, 89196576, 2629632),
-        (0, 0, 5243232, 134217729, 5243010, 9437249, -2146893816, 9764864),
-        (0, 0, 1074855936, 1086465, 1343856642, 1074860032, 65536, 1074302976),
-        (0, 0, 131074, 2097152, 65544, 65540, 1048576, 16),
-        (0, 0, 0, 0, 0, 268435457, 1073741824, 268435456),
+        (1923194619, 1858111199, 0, 0),
+        (-1337942274, 0, 0, -1878894304),
+        (50406, 16896, 6176, 265216),
+        (570425518, 402653325, 603979776, -2113929142),
+        (8947727, 135170, 0, -2146955264),
+        (-2113929023, 33280, 33685504, 164354),
+        (131584, 0, 0, 0),
+        (1073741824, 0, 0, 8388608),
+    ),
+    (
+        (0, 0, -1188287234, -1281251928),
+        (1073741824, 1280065620, -1226251028, 0),
+        (24, 1050, 18398, 32960),
+        (268435456, 33554432, -2013265684, 268435460),
+        (128, -2071953280, -2147450868, 10520704),
+        (263172, -2147483644, 69222597, 67372032),
+        (0, 262148, 67108865, 0),
+        (0, 0, 8388608, 0),
+    ),
+    (
+        (0, 8224, 1112625921, 1279541328),
+        (0, 867286947, 1090914817, 128),
+        (2560, 1074043105, 1409318913, 100663840),
+        (3072, 1627393058, 1392511489, 536871073),
+        (1073741824, 1073741825, 1393821952, 33948160),
+        (0, 268435489, 268470528, 268505585),
+        (0, 1280, 66048, 0),
+        (0, 1073741952, 1090519040, 1073741824),
     ),
 )
+LAGS = (
+    ((0, 0, 0, 0), (1644203262, 1644171005, -536905953, 536903906), (1644201084, 301992000, 1879076992, 1342210146), (2178, 1610614461, -63713, 128), (0, 2, 35040, 0)),
+    ((0, 0, 0, 0), (16843008, 73984, -16843011, 83960065), (208953344, 2088522796, 1567950110, 1549030428), (16843008, 74000, -16843011, 83960065), (0, 0, 16843008, 0)),
+    ((0, 0, 0, 0), (-50529028, 50529027, 50529024, 1128465155), (289502477, 1648517666, 1112670720, 1107456514), (-318969632, 16843009, 16843008, 1094779137), (50529027, 0, 0, 0)),
+    ((0, 0, 0, 0), (2013265907, -1946140596, -1474288388, 134219790), (1946440736, -2013265840, -1944051594, 204239900), (134212563, 67125260, 1164, 2062), (-2013265908, 0, 0, 0)),
+)
+MAXLAG = 20
+
 
 STEPS = ((1, 0, 0), (-1, 0, 0), (0, 1, 0), (0, -1, 0), (0, 0, 1), (0, 0, -1), (0, 0, 2), (0, 0, -2))
 
 
 def lookup(words, word, bit):
     value = jnp.int32(words[0])
-    for k in range(1, 8):
+    for k in range(1, 4):
         value = jnp.where(word == k, jnp.int32(words[k]), value)
     return lax.shift_right_logical(value, bit) & 1
 
@@ -154,49 +182,51 @@
 
     q_ref[...] = (jnp.dot(hidden, wq_ref[...], preferred_element_type=F32) * SCALE).astype(BF)
 
-    index = ((x * 4 + y) * 8 + z) * 2 + core
-    flags = [[lookup(TABLE[g][a], index // 32, index % 32) for a in range(8)] for g in range(2)]
-    lags = [jnp.where(x == 2, LAG, 0), jnp.where(x == 0, LAG, 0)]
-
-    def piece(band, k, g, arc, target):
-        rows = h0_ref.at[pl.ds(pl.multiple_of(band * TOK + k * CH, CH), CH)]
+    index = (x * 4 + y) * 8 + z
+    word, bit = index // 32, index % 32
+    flags = [[lookup(words, word, bit) if any(words) else None for words in ARCS[g]] for g in range(4)]
+    lags = [sum(lookup(words, word, bit) * 2**i for i, words in enumerate(LAGS[g])) for g in range(4)]
+
+    def piece(side, g, k, arc, target):
+        first = (side + 2 * (g // 2)) * TOK + (g % 2) * PART + k * CH
+        rows = h0_ref.at[pl.ds(pl.multiple_of(first, CH), CH)]
         return pltpu.make_async_remote_copy(
-            src_ref=rows, dst_ref=rows, send_sem=send.at[g, k, arc], recv_sem=recv.at[band, k],
+            src_ref=rows, dst_ref=rows, send_sem=send.at[g, k, arc], recv_sem=recv.at[side, g, k],
             device_id=target, device_id_type=MESH,
         )
 
     def slot(s, _):
-        for g in range(2):
-            band = core + 2 * g
+        for g in range(4):
             k = s - lags[g]
 
             @pl.when((k >= 0) & (k < NCH))
             def _():
-                @pl.when((f != 0) | (b != band))
+                @pl.when((f != 0) | (b != core + 2 * (g // 2)))
                 def _():
-                    piece(band, k, g, 8, partner).wait_recv()
+                    piece(core, g, k, 8, partner).wait_recv()
 
                 for a in range(8):
+                    if flags[g][a] is not None:
+                        @pl.when(flags[g][a] == 1)
+                        def _():
+                            piece(core, g, k, a, targets[a]).start()
+
+                piece(core, g, k, 8, partner).start()
+
+        return 0
+
+    lax.fori_loop(0, NCH + MAXLAG, slot, 0)
+
+    def finish(k, _):
+        for g in range(4):
+            for a in range(8):
+                if flags[g][a] is not None:
                     @pl.when(flags[g][a] == 1)
                     def _():
-                        piece(band, k, g, a, targets[a]).start()
-
-                piece(band, k, g, 8, partner).start()
-
-        return 0
-
-    lax.fori_loop(0, NCH + LAG, slot, 0)
-
-    def finish(k, _):
-        for g in range(2):
-            band = core + 2 * g
-            for a in range(8):
-                @pl.when(flags[g][a] == 1)
-                def _():
-                    piece(band, k, g, a, targets[a]).wait_send()
-
-            piece(band, k, g, 8, partner).wait_send()
-            piece(1 - core + 2 * g, k, g, 8, partner).wait_recv()
+                        piece(core, g, k, a, targets[a]).wait_send()
+
+            piece(core, g, k, 8, partner).wait_send()
+            piece(1 - core, g, k, 8, partner).wait_recv()
         return 0
 
     lax.fori_loop(0, NCH, finish, 0)
@@ -249,8 +279,8 @@
             pltpu.SemaphoreType.DMA((3,)),
             pltpu.SemaphoreType.DMA((2,)),
             pltpu.SemaphoreType.DMA((2,)),
-            pltpu.SemaphoreType.DMA((4, NCH)),
-            pltpu.SemaphoreType.DMA((2, NCH, 9)),
+            pltpu.SemaphoreType.DMA((2, 4, NCH)),
+            pltpu.SemaphoreType.DMA((4, NCH, 9)),
         ],
         compiler_params=pltpu.CompilerParams(collective_id=0, has_side_effects=True),
         name="spread",

time: 189 us -> 83.5 us (0.44)
  the two profiles are of different devices: /device:TPU:65 before, /device:TPU:17 now
where the time goes in v2:
time: 83.5 us; the launch traced here: 83.4 us
  Pallas kernels  82.1 us (98%)
  local copies, waits for them, and re-layouts  1.26 us (2%)
    pallas_call x1, Pallas kernels, per_device(): pl.pallas_call(spread_kernel, out_shape=[tokens, tokens, jax.ShapeDtypeSt...  49.8 us
    pallas_call x1, Pallas kernels, per_device(): pl.pallas_call(attend_kernel, out_shape=tokens, in_specs=[vmem] * 5, out_...  32.3 us

profile of v2, /device:TPU:17, one launch (start us, length us, event | category | flops | bytes accessed | tf_op | source)
XLA Modules:
  0.0 83.4 jit_solution(3184534249974641182)
XLA Ops:
  0.0 1.3 %reshape.14.b_ref = bf16[1,640]{1,0:T(2,128)(2,1)} reshape(bf16[640]{0:T(1024)(128)(2,1)} %param.8) | data formatting | bytes 2560 | tf_op jit(solution)/shard_map/reshape | solution.py:287
  1.3 49.8 %spread.1 = (bf16[512,640]{1,0:T(8,128)(2,1)}, bf16[512,640]{1,0:T(8,128)(2,1)}, bf16[2048,640]{1,0:T(8,128)(2,1)}) custom-call(bf16[512,640]{1,0:T(8,128)(2,1)} %bitcast.4, bf16[3,1920,640]{2,1,0:T(8,128)(2,1)} %bitcast.3, bf16[1,640]{1,0:T(2,128)(2,1)} %reshape.14.b_ref, bf16[640,640]{1,0:T(8,128)(2,1)} %wq_ref.1), custom_call_target="tpu_custom_call" | custom-call | tf_op jit(solution)/shard_map/spread/pallas_call | solution.py:269
  51.1 32.3 %attend.1 = bf16[512,640]{1,0:T(8,128)(2,1)} custom-call(bf16[512,640]{1,0:T(8,128)(2,1)} %get-tuple-element.8.h_ref, bf16[512,640]{1,0:T(8,128)(2,1)} %get-tuple-element.9.q_ref, bf16[2048,640]{1,0:T(8,128)(2,1)} %get-tuple-element.10.h0_ref, bf16[640,1280]{1,0:T(8,128)(2,1)} %wkv_ref.1, bf16[640,640]{1,0:T(8,128)(2,1)} %wout_ref.1), custom_call_target="tpu_custom_call" | custom-call | tf_op jit(solution)/shard_map/attend/pallas_call | solution.py:288

commit v3 on v2

--- a/solution.py
+++ b/solution.py
@@ -84,15 +84,17 @@
 
 def place(pad, act, row0):
     n = act.shape[0]
+    rows = slice(row0, row0 + n)
     col = lax.broadcasted_iota(jnp.int32, (n, 1), 0) % COLS
-    pad[1, row0 : row0 + n] = act.astype(BF)
-    pad[0, row0 : row0 + n] = jnp.where(col == 0, 0.0, pltpu.roll(act, 1, 0)).astype(BF)
-    pad[2, row0 : row0 + n] = jnp.where(col == COLS - 1, 0.0, pltpu.roll(act, n - 1, 0)).astype(BF)
-
-
-def spread_kernel(
-    x_ref, w_hbm, b_ref, wq_ref, hid_ref, q_ref, h0_ref,
-    wbuf, pad, halo, acc, wsem, hsend, hrecv, recv, send,
+    pad[rows, C : 2 * C] = act.astype(BF)
+    pad[rows, 0:C] = jnp.where(col == 0, 0.0, pltpu.roll(act, 1, 0)).astype(BF)
+    pad[rows, 2 * C :] = jnp.where(col == COLS - 1, 0.0, pltpu.roll(act, n - 1, 0)).astype(BF)
+
+
+def block_kernel(
+    x_hbm, w_hbm, b_ref, wq_hbm, wkv_hbm, wout_hbm, o_ref,
+    x_ref, wbuf, wq_ref, wkv_ref, wout_ref, pad, halo, acc, hid_ref, q_ref, h0_ref, kv, mix,
+    sems, hsend, hrecv, recv, send,
 ):
     f = lax.axis_index("frame")
     b = lax.axis_index("band")
@@ -108,9 +110,16 @@
     targets = [chip(step) for step in STEPS]
     partner = (f, b + 1 - 2 * core)
 
-    weights = [pltpu.make_async_copy(w_hbm.at[i], wbuf.at[i], wsem.at[i]) for i in range(3)]
+    load_x = pltpu.make_async_copy(x_hbm, x_ref, sems.at[3])
+    load_x.start()
+    weights = [pltpu.make_async_copy(w_hbm.at[i], wbuf.at[i], sems.at[i]) for i in range(3)]
     for i in (1, 0, 2):
         weights[i].start()
+    load_q = pltpu.make_async_copy(wq_hbm, wq_ref, sems.at[4])
+    load_kv = pltpu.make_async_copy(wkv_hbm, wkv_ref, sems.at[5])
+    load_out = pltpu.make_async_copy(wout_hbm, wout_ref, sems.at[6])
+    for load in (load_q, load_kv, load_out):
+        load.start()
 
     barrier = pltpu.get_barrier_semaphore()
     for target in targets + [partner]:
@@ -121,6 +130,8 @@
     def _():
         pl.semaphore_signal(barrier, inc=1, device_id=(f, 3 - b), device_id_type=MESH)
 
+    load_x.wait()
+    place(pad, silu(x_ref[...]), COLS)
     pl.semaphore_wait(barrier, jnp.where(middle, 10, 9))
 
     def halo_copy(rows, slot, target):
@@ -141,15 +152,11 @@
     def _():
         down.start()
 
-    place(pad, silu(x_ref[...]), COLS)
-    acc[...] = x_ref[...].astype(F32) + b_ref[...].astype(F32)
-
-    def tap(i):
-        weights[i].wait()
-        window = jnp.concatenate([pad[c, i * COLS : i * COLS + TOK] for c in range(3)], axis=1)
-        acc[...] += jnp.dot(window, wbuf[i], preferred_element_type=F32)
-
-    tap(1)
+    weights[1].wait()
+    acc[...] = (
+        x_ref[...].astype(F32) + b_ref[...].astype(F32)
+        + jnp.dot(pad[COLS : COLS + TOK], wbuf[1], preferred_element_type=F32)
+    )
 
     @pl.when(b > 0)
     def _():
@@ -159,7 +166,7 @@
 
     @pl.when(b == 0)
     def _():
-        pad[:, 0:COLS] = jnp.zeros((3, COLS, C), BF)
+        pad[0:COLS] = jnp.zeros((COLS, 3 * C), BF)
 
     @pl.when(b < 3)
     def _():
@@ -169,18 +176,23 @@
 
     @pl.when(b == 3)
     def _():
-        pad[:, TOK + COLS :] = jnp.zeros((3, COLS, C), BF)
-
-    tap(0)
-    tap(2)
-    hidden = acc[...].astype(BF)
+        pad[TOK + COLS :] = jnp.zeros((COLS, 3 * C), BF)
+
+    weights[0].wait()
+    weights[2].wait()
+    hidden = (
+        acc[...] + jnp.dot(pad[0:TOK], wbuf[0], preferred_element_type=F32)
+        + jnp.dot(pad[2 * COLS :], wbuf[2], preferred_element_type=F32)
+    ).astype(BF)
     hid_ref[...] = hidden
 
     @pl.when(f == 0)
     def _():
         h0_ref[pl.ds(pl.multiple_of(b * TOK, TOK), TOK), :] = hidden
 
+    load_q.wait()
     q_ref[...] = (jnp.dot(hidden, wq_ref[...], preferred_element_type=F32) * SCALE).astype(BF)
+    kv[:, :, 256:] = jnp.ones((5, KEYS, 128), BF)
 
     index = (x * 4 + y) * 8 + z
     word, bit = index // 32, index % 32
@@ -217,6 +229,52 @@
 
     lax.fori_loop(0, NCH + MAXLAG, slot, 0)
 
+    load_kv.wait()
+    load_out.wait()
+
+    def project(band):
+        rows = pl.ds(pl.multiple_of(band * TOK, TOK), TOK)
+        both = jnp.dot(h0_ref[rows, :], wkv_ref[...], preferred_element_type=F32).astype(BF)
+        for j in range(5):
+            kv[j, rows, 0:128] = both[:, j * 128 : (j + 1) * 128]
+            kv[j, rows, 128:256] = both[:, C + j * 128 : C + (j + 1) * 128]
+
+    def own(i, _):
+        project(core + 2 * i)
+        return 0
+
+    lax.fori_loop(0, 2, own, 0)
+
+    def other(i, _):
+        def arrive(k, _):
+            for h in range(2):
+                piece(1 - core, 2 * i + h, k, 8, partner).wait_recv()
+            return 0
+
+        lax.fori_loop(0, NCH, arrive, 0)
+        project(1 - core + 2 * i)
+        return 0
+
+    lax.fori_loop(0, 2, other, 0)
+
+    lane = lax.broadcasted_iota(jnp.int32, (1, 128), 1)
+    for j in range(5):
+        columns = slice(j * 128, (j + 1) * 128)
+        outs = []
+        for half in range(2):
+            keep = (lane < 64) if half == 0 else (lane >= 64)
+            head = jnp.where(keep, q_ref[:, columns], jnp.zeros((), BF))
+            scores = lax.dot_general(head, kv[j, :, 0:128], (((1,), (1,)), ((), ())), preferred_element_type=F32)
+            best = jnp.max(scores, axis=1, keepdims=True)
+            prob = jnp.exp2(scores - best).astype(BF)
+            out = jnp.dot(prob, kv[j, :, 128:384], preferred_element_type=F32)
+            outs.append(out[:, :128] / out[:, 128:])
+        mix[:, columns] = jnp.where(lane < 64, outs[0], outs[1]).astype(BF)
+
+    o_ref[...] = (
+        hid_ref[...].astype(F32) + jnp.dot(mix[...], wout_ref[...], preferred_element_type=F32)
+    ).astype(BF)
+
     def finish(k, _):
         for g in range(4):
             for a in range(8):
@@ -226,77 +284,42 @@
                         piece(core, g, k, a, targets[a]).wait_send()
 
             piece(core, g, k, 8, partner).wait_send()
-            piece(1 - core, g, k, 8, partner).wait_recv()
         return 0
 
     lax.fori_loop(0, NCH, finish, 0)
-
-
-def attend_kernel(h_ref, q_ref, h0_ref, wkv_ref, wout_ref, o_ref, keys, values, mix):
-    lane = lax.broadcasted_iota(jnp.int32, (1, 128), 1)
-    values[:, 128:] = jnp.ones((KEYS, 128), BF)
-    block = 128
-
-    @pl.loop(0, 5)
-    def _(j):
-        c = pl.multiple_of(j * 128, 128)
-        w = jnp.concatenate([wkv_ref[:, pl.ds(c, 128)], wkv_ref[:, pl.ds(pl.multiple_of(C + c, 128), 128)]], axis=1)
-        kv = jnp.dot(h0_ref[...], w, preferred_element_type=F32).astype(BF)
-        keys[...] = kv[:, :128]
-        values[:, :128] = kv[:, 128:]
-        for half in range(2):
-            keep = (lane < 64) if half == 0 else (lane >= 64)
-            for r in range(TOK // block):
-                rows = slice(r * block, (r + 1) * block)
-                head = jnp.where(keep, q_ref[rows, pl.ds(c, 128)], jnp.zeros((), BF))
-                scores = lax.dot_general(head, keys[...], (((1,), (1,)), ((), ())), preferred_element_type=F32)
-                best = jnp.max(scores, axis=1, keepdims=True)
-                prob = jnp.exp2(scores - best).astype(BF)
-                out = jnp.dot(prob, values[...], preferred_element_type=F32)
-                out = (out[:, :128] / out[:, 128:]).astype(BF)
-                if half == 1:
-                    out = jnp.where(keep, out, mix[rows, pl.ds(c, 128)])
-                mix[rows, pl.ds(c, 128)] = out
-
-    o_ref[...] = (
-        h_ref[...].astype(F32) + jnp.dot(mix[...], wout_ref[...], preferred_element_type=F32)
-    ).astype(BF)
 
 
 def per_device(latents, conv_weight, conv_bias, w_query, w_keyval, w_out):
     vmem = pl.BlockSpec(memory_space=pltpu.VMEM)
-    tokens = jax.ShapeDtypeStruct((TOK, C), BF)
-    hidden, queries, first = pl.pallas_call(
-        spread_kernel,
-        out_shape=[tokens, tokens, jax.ShapeDtypeStruct((KEYS, C), BF)],
-        in_specs=[vmem, pl.BlockSpec(memory_space=pl.ANY), vmem, vmem],
-        out_specs=[vmem, vmem, vmem],
+    hbm = pl.BlockSpec(memory_space=pl.ANY)
+    result = pl.pallas_call(
+        block_kernel,
+        out_shape=jax.ShapeDtypeStruct((TOK, C), BF),
+        in_specs=[hbm, hbm, vmem, hbm, hbm, hbm],
+        out_specs=vmem,
         scratch_shapes=[
+            pltpu.VMEM((TOK, C), BF),
             pltpu.VMEM((3, 3 * C, C), BF),
-            pltpu.VMEM((3, TOK + 2 * COLS, C), BF),
+            pltpu.VMEM((C, C), BF),
+            pltpu.VMEM((C, 2 * C), BF),
+            pltpu.VMEM((C, C), BF),
+            pltpu.VMEM((TOK + 2 * COLS, 3 * C), BF),
             pltpu.VMEM((2, COLS, C), BF),
             pltpu.VMEM((TOK, C), F32),
-            pltpu.SemaphoreType.DMA((3,)),
+            pltpu.VMEM((TOK, C), BF),
+            pltpu.VMEM((TOK, C), BF),
+            pltpu.VMEM((KEYS, C), BF),
+            pltpu.VMEM((5, KEYS, 384), BF),
+            pltpu.VMEM((TOK, C), BF),
+            pltpu.SemaphoreType.DMA((7,)),
             pltpu.SemaphoreType.DMA((2,)),
             pltpu.SemaphoreType.DMA((2,)),
             pltpu.SemaphoreType.DMA((2, 4, NCH)),
             pltpu.SemaphoreType.DMA((4, NCH, 9)),
         ],
         compiler_params=pltpu.CompilerParams(collective_id=0, has_side_effects=True),
-        name="spread",
-    )(latents.reshape(TOK, C), conv_weight.reshape(3, 3 * C, C), conv_bias.reshape(1, C), w_query)
-    result = pl.pallas_call(
-        attend_kernel,
-        out_shape=tokens,
-        in_specs=[vmem] * 5,
-        out_specs=vmem,
-        scratch_shapes=[
-            pltpu.VMEM((KEYS, 128), BF),
-            pltpu.VMEM((KEYS, 256), BF),
-            pltpu.VMEM((TOK, C), BF),
-        ],
-        name="attend",
-    )(hidden, queries, first, w_keyval, w_out)
+        name="block",
+    )(latents.reshape(TOK, C), conv_weight.reshape(3, 3 * C, C), conv_bias, w_query, w_keyval, w_out)
     return result.reshape(latents.shape)
 
 

time: 83.5 us -> 67 us (0.80)
  Pallas kernels: 82.1 us -> 64.6 us
    pallas_call x2 -> x1, Pallas kernels: 82.1 us -> 64.6 us  [per_device(): pl.pallas_call(block_kernel, out_shape=jax.ShapeDtypeStruct((TOK, C), BF)...]
    unnamed x0 -> x1, local copies, waits for them, and re-layouts: none -> 1.98 us
    reshape x1 -> x0, local copies, waits for them, and re-layouts: 1.26 us -> none  [per_device(): conv_bias.reshape(1, C)]
where the time goes in v3:
time: 67 us; the launch traced here: 66.6 us
  Pallas kernels  64.6 us (96%)
  local copies, waits for them, and re-layouts  1.98 us (3%)
    pallas_call x1, Pallas kernels, per_device(): pl.pallas_call(block_kernel, out_shape=jax.ShapeDtypeStruct((TOK, C), BF)...  64.6 us
    unnamed x1, local copies, waits for them, and re-layouts  1.98 us

profile of v3, /device:TPU:17, one launch (start us, length us, event | category | flops | bytes accessed | tf_op | source)
XLA Modules:
  0.0 66.6 jit_solution(8607943891391487576)
XLA Ops:
  0.0 64.6 %block.1 = bf16[512,640]{1,0:T(8,128)(2,1)} custom-call(bf16[512,640]{1,0:T(8,128)(2,1)} %bitcast.5, bf16[3,1920,640]{2,1,0:T(8,128)(2,1)} %bitcast.3, bf16[640]{0:T(1024)(128)(2,1)} %b_ref.1, bf16[640,640]{1,0:T(8,128)(2,1)} %wq_hbm.1, bf16[640,1280]{1,0:T(8,128)(2,1)} %wkv_hbm.1, bf16[640,640]{1,0:T(8,128)(2,1)} %wout_hbm.1), custom_call_target="tpu_custom_call" | custom-call | tf_op jit(solution)/shard_map/block/pallas_call | solution.py:295
  64.6 2.0 %copy.8 = bf16[1,16,32,640]{3,2,1,0:T(8,128)(2,1)} copy(bf16[1,16,32,640]{3,2,1,0:T(8,128)(2,1)} %bitcast.4) | data formatting | bytes 1310720

commit v4 on v3

--- a/solution.py
+++ b/solution.py
@@ -1,3 +1,5 @@
+import functools
+
 import jax
 import jax.numpy as jnp
 from jax import lax
@@ -11,11 +13,23 @@
 ROWS, COLS, C = 16, 32, 640
 TOK = ROWS * COLS
 KEYS = 4 * TOK
+NT = 2
 NCH = 8
-PART = TOK // 2
-CH = PART // NCH
+HALF = NCH // 2
+PART = TOK // 4
+CH = PART // HALF
 SCALE = 0.125 * 1.4426950408889634
 
+STEPS = (
+    (1, 0, 0),
+    (-1, 0, 0),
+    (0, 1, 0),
+    (0, -1, 0),
+    (0, 0, 1),
+    (0, 0, -1),
+    (0, 0, 2),
+    (0, 0, -2),
+)
 ARCS = (
     (
         (157049088, -1860284160, 0, 4),
@@ -67,9 +81,6 @@
 MAXLAG = 20
 
 
-STEPS = ((1, 0, 0), (-1, 0, 0), (0, 1, 0), (0, -1, 0), (0, 0, 1), (0, 0, -1), (0, 0, 2), (0, 0, -2))
-
-
 def lookup(words, word, bit):
     value = jnp.int32(words[0])
     for k in range(1, 4):
@@ -94,7 +105,7 @@
 def block_kernel(
     x_hbm, w_hbm, b_ref, wq_hbm, wkv_hbm, wout_hbm, o_ref,
     x_ref, wbuf, wq_ref, wkv_ref, wout_ref, pad, halo, acc, hid_ref, q_ref, h0_ref, kv, mix,
-    sems, hsend, hrecv, recv, send,
+    sems, hsend, hrecv, recv, send, psend, precv,
 ):
     f = lax.axis_index("frame")
     b = lax.axis_index("band")
@@ -132,7 +143,7 @@
 
     load_x.wait()
     place(pad, silu(x_ref[...]), COLS)
-    pl.semaphore_wait(barrier, jnp.where(middle, 10, 9))
+    pl.semaphore_wait(barrier, len(targets) + 1 + middle.astype(jnp.int32))
 
     def halo_copy(rows, slot, target):
         return pltpu.make_async_remote_copy(
@@ -178,57 +189,94 @@
     def _():
         pad[TOK + COLS :] = jnp.zeros((COLS, 3 * C), BF)
 
+    index = (x * 4 + y) * 8 + z
+    word, bit = index // 32, index % 32
+    flags = [[lookup(words, word, bit) if any(words) else None for words in ARCS[g]] for g in range(2 * NT)]
+    lags = [sum(lookup(words, word, bit) * 2**i for i, words in enumerate(LAGS[g])) for g in range(2 * NT)]
+
+    def part_row(side, g, half):
+        return (side + 2 * lax.div(g, NT)) * TOK + half * (2 * PART) + lax.rem(g, NT) * PART
+
+    def piece(side, g, k, arc, target):
+        first = part_row(side, g, lax.div(k, HALF)) + lax.rem(k, HALF) * CH
+        rows = h0_ref.at[pl.ds(pl.multiple_of(first, CH), CH)]
+        return pltpu.make_async_remote_copy(
+            src_ref=rows, dst_ref=rows, send_sem=send.at[g, k, arc], recv_sem=recv.at[g, k],
+            device_id=target, device_id_type=MESH,
+        )
+
+    def share(side, g, half):
+        rows = h0_ref.at[pl.ds(pl.multiple_of(part_row(side, g, half), PART), PART)]
+        return pltpu.make_async_remote_copy(
+            src_ref=rows, dst_ref=rows, send_sem=psend.at[g, half], recv_sem=precv.at[g, half],
+            device_id=partner, device_id_type=MESH,
+        )
+
+    def forward(g, k):
+        for a in range(len(STEPS)):
+            if flags[g][a] is not None:
+                @pl.when(flags[g][a] == 1)
+                def _():
+                    piece(core, g, k, a, targets[a]).start()
+
+        for half in range(2):
+            @pl.when(k == half * HALF + HALF - 1)
+            def _():
+                share(core, g, half).start()
+
+    def early(i):
+        def send_one(k, _):
+            for h in range(NT):
+                forward(NT * i + h, k)
+            return 0
+
+        lax.fori_loop(0, HALF, send_one, 0)
+
     weights[0].wait()
     weights[2].wait()
-    hidden = (
-        acc[...] + jnp.dot(pad[0:TOK], wbuf[0], preferred_element_type=F32)
-        + jnp.dot(pad[2 * COLS :], wbuf[2], preferred_element_type=F32)
-    ).astype(BF)
-    hid_ref[...] = hidden
-
-    @pl.when(f == 0)
-    def _():
-        h0_ref[pl.ds(pl.multiple_of(b * TOK, TOK), TOK), :] = hidden
+    block = TOK // 2
+    for half in range(2):
+        top = half * block
+        rows = slice(top, top + block)
+        hidden = (
+            acc[rows] + jnp.dot(pad[rows], wbuf[0], preferred_element_type=F32)
+            + jnp.dot(pad[top + 2 * COLS : top + 2 * COLS + block], wbuf[2], preferred_element_type=F32)
+        ).astype(BF)
+        hid_ref[rows] = hidden
+
+        @pl.when(f == 0)
+        def _():
+            h0_ref[pl.ds(pl.multiple_of(b * TOK + top, block), block), :] = hidden
+            if half == 0:
+                for i in range(2):
+                    pl.when(b == core + 2 * i)(functools.partial(early, i))
 
     load_q.wait()
-    q_ref[...] = (jnp.dot(hidden, wq_ref[...], preferred_element_type=F32) * SCALE).astype(BF)
-    kv[:, :, 256:] = jnp.ones((5, KEYS, 128), BF)
-
-    index = (x * 4 + y) * 8 + z
-    word, bit = index // 32, index % 32
-    flags = [[lookup(words, word, bit) if any(words) else None for words in ARCS[g]] for g in range(4)]
-    lags = [sum(lookup(words, word, bit) * 2**i for i, words in enumerate(LAGS[g])) for g in range(4)]
-
-    def piece(side, g, k, arc, target):
-        first = (side + 2 * (g // 2)) * TOK + (g % 2) * PART + k * CH
-        rows = h0_ref.at[pl.ds(pl.multiple_of(first, CH), CH)]
-        return pltpu.make_async_remote_copy(
-            src_ref=rows, dst_ref=rows, send_sem=send.at[g, k, arc], recv_sem=recv.at[side, g, k],
-            device_id=target, device_id_type=MESH,
-        )
+
+    def prepare():
+        q_ref[...] = (jnp.dot(hid_ref[...], wq_ref[...], preferred_element_type=F32) * SCALE).astype(BF)
+        kv[:, :, 256:] = jnp.ones((5, KEYS, 128), BF)
+
+    pl.when(f != 0)(prepare)
 
     def slot(s, _):
-        for g in range(4):
+        for g in range(2 * NT):
             k = s - lags[g]
-
-            @pl.when((k >= 0) & (k < NCH))
+            source = (f == 0) & (b == core + 2 * (g // NT))
+
+            @pl.when((k >= 0) & (k < NCH) & jnp.logical_not(source & (k < HALF)))
             def _():
-                @pl.when((f != 0) | (b != core + 2 * (g // 2)))
+                @pl.when(jnp.logical_not(source))
                 def _():
-                    piece(core, g, k, 8, partner).wait_recv()
-
-                for a in range(8):
-                    if flags[g][a] is not None:
-                        @pl.when(flags[g][a] == 1)
-                        def _():
-                            piece(core, g, k, a, targets[a]).start()
-
-                piece(core, g, k, 8, partner).start()
+                    piece(core, g, k, 0, partner).wait_recv()
+
+                forward(g, k)
 
         return 0
 
     lax.fori_loop(0, NCH + MAXLAG, slot, 0)
 
+    pl.when(f == 0)(prepare)
     load_kv.wait()
     load_out.wait()
 
@@ -246,12 +294,9 @@
     lax.fori_loop(0, 2, own, 0)
 
     def other(i, _):
-        def arrive(k, _):
-            for h in range(2):
-                piece(1 - core, 2 * i + h, k, 8, partner).wait_recv()
-            return 0
-
-        lax.fori_loop(0, NCH, arrive, 0)
+        for h in range(NT):
+            for half in range(2):
+                share(1 - core, NT * i + h, half).wait_recv()
         project(1 - core + 2 * i)
         return 0
 
@@ -276,17 +321,19 @@
     ).astype(BF)
 
     def finish(k, _):
-        for g in range(4):
-            for a in range(8):
+        for g in range(2 * NT):
+            for a in range(len(STEPS)):
                 if flags[g][a] is not None:
                     @pl.when(flags[g][a] == 1)
                     def _():
                         piece(core, g, k, a, targets[a]).wait_send()
 
-            piece(core, g, k, 8, partner).wait_send()
         return 0
 
     lax.fori_loop(0, NCH, finish, 0)
+    for g in range(2 * NT):
+        for half in range(2):
+            share(core, g, half).wait_send()
 
 
 def per_device(latents, conv_weight, conv_bias, w_query, w_keyval, w_out):
@@ -314,8 +361,10 @@
             pltpu.SemaphoreType.DMA((7,)),
             pltpu.SemaphoreType.DMA((2,)),
             pltpu.SemaphoreType.DMA((2,)),
-            pltpu.SemaphoreType.DMA((2, 4, NCH)),
-            pltpu.SemaphoreType.DMA((4, NCH, 9)),
+            pltpu.SemaphoreType.DMA((2 * NT, NCH)),
+            pltpu.SemaphoreType.DMA((2 * NT, NCH, len(STEPS))),
+            pltpu.SemaphoreType.DMA((2 * NT, 2)),
+            pltpu.SemaphoreType.DMA((2 * NT, 2)),
         ],
         compiler_params=pltpu.CompilerParams(collective_id=0, has_side_effects=True),
         name="block",

time: 67 us -> 64 us (0.955)
  Pallas kernels: 64.6 us -> 61.3 us
    pallas_call x1, Pallas kernels: 64.6 us -> 61.3 us  [per_device(): pl.pallas_call(block_kernel, out_shape=jax.ShapeDtypeStruct((TOK, C), BF)...]
where the time goes in v4:
time: 64 us; the launch traced here: 63.3 us
  Pallas kernels  61.3 us (96%)
  local copies, waits for them, and re-layouts  1.98 us (3%)
    pallas_call x1, Pallas kernels, per_device(): pl.pallas_call(block_kernel, out_shape=jax.ShapeDtypeStruct((TOK, C), BF)...  61.3 us
    unnamed x1, local copies, waits for them, and re-layouts  1.98 us

profile of v4, /device:TPU:17, one launch (start us, length us, event | category | flops | bytes accessed | tf_op | source)
XLA Modules:
  0.0 63.3 jit_solution(2969717471700104695)
XLA Ops:
  0.0 61.3 %block.1 = bf16[512,640]{1,0:T(8,128)(2,1)} custom-call(bf16[512,640]{1,0:T(8,128)(2,1)} %bitcast.5, bf16[3,1920,640]{2,1,0:T(8,128)(2,1)} %bitcast.3, bf16[640]{0:T(1024)(128)(2,1)} %b_ref.1, bf16[640,640]{1,0:T(8,128)(2,1)} %wq_hbm.1, bf16[640,1280]{1,0:T(8,128)(2,1)} %wkv_hbm.1, bf16[640,640]{1,0:T(8,128)(2,1)} %wout_hbm.1), custom_call_target="tpu_custom_call" | custom-call | tf_op jit(solution)/shard_map/block/pallas_call | solution.py:342
  61.3 2.0 %copy.8 = bf16[1,16,32,640]{3,2,1,0:T(8,128)(2,1)} copy(bf16[1,16,32,640]{3,2,1,0:T(8,128)(2,1)} %bitcast.4) | data formatting | bytes 1310720

commit v5 on v4

--- a/solution.py
+++ b/solution.py
@@ -16,6 +16,7 @@
 NT = 2
 NCH = 8
 HALF = NCH // 2
+DELTA = 2
 PART = TOK // 4
 CH = PART // HALF
 SCALE = 0.125 * 1.4426950408889634
@@ -103,8 +104,8 @@
 
 
 def block_kernel(
-    x_hbm, w_hbm, b_ref, wq_hbm, wkv_hbm, wout_hbm, o_ref,
-    x_ref, wbuf, wq_ref, wkv_ref, wout_ref, pad, halo, acc, hid_ref, q_ref, h0_ref, kv, mix,
+    x_ref, w_hbm, b_ref, wq_hbm, wkv_hbm, wout_hbm, o_ref,
+    wbuf, wq_ref, wkv_ref, wout_ref, pad, halo, acc, hid_ref, q_ref, h0_ref, kv, mix,
     sems, hsend, hrecv, recv, send, psend, precv,
 ):
     f = lax.axis_index("frame")
@@ -121,14 +122,12 @@
     targets = [chip(step) for step in STEPS]
     partner = (f, b + 1 - 2 * core)
 
-    load_x = pltpu.make_async_copy(x_hbm, x_ref, sems.at[3])
-    load_x.start()
     weights = [pltpu.make_async_copy(w_hbm.at[i], wbuf.at[i], sems.at[i]) for i in range(3)]
     for i in (1, 0, 2):
         weights[i].start()
-    load_q = pltpu.make_async_copy(wq_hbm, wq_ref, sems.at[4])
-    load_kv = pltpu.make_async_copy(wkv_hbm, wkv_ref, sems.at[5])
-    load_out = pltpu.make_async_copy(wout_hbm, wout_ref, sems.at[6])
+    load_q = pltpu.make_async_copy(wq_hbm, wq_ref, sems.at[3])
+    load_kv = pltpu.make_async_copy(wkv_hbm, wkv_ref, sems.at[4])
+    load_out = pltpu.make_async_copy(wout_hbm, wout_ref, sems.at[5])
     for load in (load_q, load_kv, load_out):
         load.start()
 
@@ -141,7 +140,6 @@
     def _():
         pl.semaphore_signal(barrier, inc=1, device_id=(f, 3 - b), device_id_type=MESH)
 
-    load_x.wait()
     place(pad, silu(x_ref[...]), COLS)
     pl.semaphore_wait(barrier, len(targets) + 1 + middle.astype(jnp.int32))
 
@@ -259,6 +257,17 @@
 
     pl.when(f != 0)(prepare)
 
+    load_kv.wait()
+
+    def project(side, g):
+        low, high = [pl.ds(pl.multiple_of(part_row(side, g, half), PART), PART) for half in range(2)]
+        rows = jnp.concatenate([h0_ref[low, :], h0_ref[high, :]], axis=0)
+        both = jnp.dot(rows, wkv_ref[...], preferred_element_type=F32).astype(BF)
+        for j in range(5):
+            pair = jnp.concatenate([both[:, j * 128 : (j + 1) * 128], both[:, C + j * 128 : C + (j + 1) * 128]], axis=1)
+            kv[j, low, 0:256] = pair[:PART]
+            kv[j, high, 0:256] = pair[PART:]
+
     def slot(s, _):
         for g in range(2 * NT):
             k = s - lags[g]
@@ -272,35 +281,37 @@
 
                 forward(g, k)
 
+        ends = [s - lags[g] - NCH for g in range(2 * NT)]
+        due = sum((e == -1).astype(jnp.int32) + (e == DELTA).astype(jnp.int32) for e in ends)
+
+        @pl.when(due > 0)
+        def _():
+            def one(t, _):
+                g = lax.rem(t, 2 * NT)
+                late = t >= 2 * NT
+                end = ends[0]
+                for h in range(1, 2 * NT):
+                    end = jnp.where(g == h, ends[h], end)
+
+                @pl.when(end == jnp.where(late, DELTA, -1))
+                def _():
+                    @pl.when(late)
+                    def _():
+                        for half in range(2):
+                            share(1 - core, g, half).wait_recv()
+
+                    project(jnp.where(late, 1 - core, core), g)
+
+                return 0
+
+            lax.fori_loop(0, 4 * NT, one, 0)
+
         return 0
 
-    lax.fori_loop(0, NCH + MAXLAG, slot, 0)
+    lax.fori_loop(0, NCH + MAXLAG + DELTA + 1, slot, 0)
 
     pl.when(f == 0)(prepare)
-    load_kv.wait()
     load_out.wait()
-
-    def project(band):
-        rows = pl.ds(pl.multiple_of(band * TOK, TOK), TOK)
-        both = jnp.dot(h0_ref[rows, :], wkv_ref[...], preferred_element_type=F32).astype(BF)
-        for j in range(5):
-            kv[j, rows, 0:128] = both[:, j * 128 : (j + 1) * 128]
-            kv[j, rows, 128:256] = both[:, C + j * 128 : C + (j + 1) * 128]
-
-    def own(i, _):
-        project(core + 2 * i)
-        return 0
-
-    lax.fori_loop(0, 2, own, 0)
-
-    def other(i, _):
-        for h in range(NT):
-            for half in range(2):
-                share(1 - core, NT * i + h, half).wait_recv()
-        project(1 - core + 2 * i)
-        return 0
-
-    lax.fori_loop(0, 2, other, 0)
 
     lane = lax.broadcasted_iota(jnp.int32, (1, 128), 1)
     for j in range(5):
@@ -342,10 +353,9 @@
     result = pl.pallas_call(
         block_kernel,
         out_shape=jax.ShapeDtypeStruct((TOK, C), BF),
-        in_specs=[hbm, hbm, vmem, hbm, hbm, hbm],
+        in_specs=[vmem, hbm, vmem, hbm, hbm, hbm],
         out_specs=vmem,
         scratch_shapes=[
-            pltpu.VMEM((TOK, C), BF),
             pltpu.VMEM((3, 3 * C, C), BF),
             pltpu.VMEM((C, C), BF),
             pltpu.VMEM((C, 2 * C), BF),
@@ -358,7 +368,7 @@
             pltpu.VMEM((KEYS, C), BF),
             pltpu.VMEM((5, KEYS, 384), BF),
             pltpu.VMEM((TOK, C), BF),
-            pltpu.SemaphoreType.DMA((7,)),
+            pltpu.SemaphoreType.DMA((6,)),
             pltpu.SemaphoreType.DMA((2,)),
             pltpu.SemaphoreType.DMA((2,)),
             pltpu.SemaphoreType.DMA((2 * NT, NCH)),
@@ -366,7 +376,7 @@
             pltpu.SemaphoreType.DMA((2 * NT, 2)),
             pltpu.SemaphoreType.DMA((2 * NT, 2)),
         ],
-        compiler_params=pltpu.CompilerParams(collective_id=0, has_side_effects=True),
+        compiler_params=pltpu.CompilerParams(collective_id=0, has_side_effects=True, vmem_limit_bytes=52 << 20),
         name="block",
     )(latents.reshape(TOK, C), conv_weight.reshape(3, 3 * C, C), conv_bias, w_query, w_keyval, w_out)
     return result.reshape(latents.shape)

time: 64 us -> 60.8 us (0.950)
  Pallas kernels: 61.3 us -> 58.1 us
    pallas_call x1, Pallas kernels: 61.3 us -> 58.1 us  [per_device(): pl.pallas_call(block_kernel, out_shape=jax.ShapeDtypeStruct((TOK, C), BF)...]
    unnamed x1 -> x5, local copies, waits for them, and re-layouts: 1.98 us -> 2.61 us
where the time goes in v5:
time: 60.8 us; the launch traced here: 60.7 us
  Pallas kernels  58.1 us (96%)
  local copies, waits for them, and re-layouts  2.61 us (4%)
    pallas_call x1, Pallas kernels, per_device(): pl.pallas_call(block_kernel, out_shape=jax.ShapeDtypeStruct((TOK, C), BF)...  58.1 us
    unnamed x5, local copies, waits for them, and re-layouts  2.61 us

profile of v5, /device:TPU:17, one launch (start us, length us, event | category | flops | bytes accessed | tf_op | source)
XLA Modules:
  0.0 60.7 jit_solution(13152829673793667636)
XLA Ops:
  0.0 0.0 copy-start
  0.0 1.1 %copy-done = bf16[1,16,32,640]{3,2,1,0:T(8,128)(2,1)S(1)} copy-done((bf16[1,16,32,640]{3,2,1,0:T(8,128)(2,1)S(1)}, bf16[1,16,32,640]{3,2,1,0:T(8,128)(2,1)}, u32[]{:S(2)}) %copy-start) | copy-done | bytes 655384
  1.1 0.0 copy-start.1
  1.1 0.7 %copy-done.1 = bf16[640]{0:T(1024)(128)(2,1)S(1)} copy-done((bf16[640]{0:T(1024)(128)(2,1)S(1)}, bf16[640]{0:T(1024)(128)(2,1)}, u32[]{:S(2)}) %copy-start.1) | copy-done | bytes 1304
  1.8 58.1 %block.1 = bf16[512,640]{1,0:T(8,128)(2,1)S(1)} custom-call(bf16[512,640]{1,0:T(8,128)(2,1)S(1)} %bitcast.4, bf16[3,1920,640]{2,1,0:T(8,128)(2,1)} %bitcast.5, bf16[640]{0:T(1024)(128)(2,1)S(1)} %copy-done.1, bf16[640,640]{1,0:T(8,128)(2,1)} %wq_hbm.1, bf16[640,1280]{1,0:T(8,128)(2,1)} %wkv_hbm.1, bf16[640,640]{1,0:T(8,128)(2,1)} %wout_hbm.1), custom_call_target="tpu_custom_call" | custom-call | tf_op jit(solution)/shard_map/block/pallas_call | solution.py:353
  59.9 0.8 %copy.8 = bf16[1,16,32,640]{3,2,1,0:T(8,128)(2,1)} copy(bf16[1,16,32,640]{3,2,1,0:T(8,128)(2,1)S(1)} %bitcast.3) | data formatting | bytes 1310720
Async XLA Ops:
  0.0 1.1 %copy-start = (bf16[1,16,32,640]{3,2,1,0:T(8,128)(2,1)S(1)}, bf16[1,16,32,640]{3,2,1,0:T(8,128)(2,1)}, u32[]{:S(2)}) copy-start(bf16[1,16,32,640]{3,2,1,0:T(8,128)(2,1)} %param.6) | copy-start | bytes 1966084
  1.1 0.7 %copy-start.1 = (bf16[640]{0:T(1024)(128)(2,1)S(1)}, bf16[640]{0:T(1024)(128)(2,1)}, u32[]{:S(2)}) copy-start(bf16[640]{0:T(1024)(128)(2,1)} %b_ref.1) | copy-start | bytes 3844

commit v6 on v5

--- a/solution.py
+++ b/solution.py
@@ -199,7 +199,7 @@
         first = part_row(side, g, lax.div(k, HALF)) + lax.rem(k, HALF) * CH
         rows = h0_ref.at[pl.ds(pl.multiple_of(first, CH), CH)]
         return pltpu.make_async_remote_copy(
-            src_ref=rows, dst_ref=rows, send_sem=send.at[g, k, arc], recv_sem=recv.at[g, k],
+            src_ref=rows, dst_ref=rows, send_sem=send.at[g, arc], recv_sem=recv.at[g, k],
             device_id=target, device_id_type=MESH,
         )
 
@@ -331,17 +331,17 @@
         hid_ref[...].astype(F32) + jnp.dot(mix[...], wout_ref[...], preferred_element_type=F32)
     ).astype(BF)
 
-    def finish(k, _):
-        for g in range(2 * NT):
-            for a in range(len(STEPS)):
-                if flags[g][a] is not None:
-                    @pl.when(flags[g][a] == 1)
-                    def _():
-                        piece(core, g, k, a, targets[a]).wait_send()
-
-        return 0
-
-    lax.fori_loop(0, NCH, finish, 0)
+    whole = h0_ref.at[pl.ds(0, 2 * PART)]
+    for g in range(2 * NT):
+        for a in range(len(STEPS)):
+            if flags[g][a] is not None:
+                @pl.when(flags[g][a] == 1)
+                def _():
+                    pltpu.make_async_remote_copy(
+                        src_ref=whole, dst_ref=whole, send_sem=send.at[g, a], recv_sem=recv.at[g, 0],
+                        device_id=targets[a], device_id_type=MESH,
+                    ).wait_send()
+
     for g in range(2 * NT):
         for half in range(2):
             share(core, g, half).wait_send()
@@ -372,7 +372,7 @@
             pltpu.SemaphoreType.DMA((2,)),
             pltpu.SemaphoreType.DMA((2,)),
             pltpu.SemaphoreType.DMA((2 * NT, NCH)),
-            pltpu.SemaphoreType.DMA((2 * NT, NCH, len(STEPS))),
+            pltpu.SemaphoreType.DMA((2 * NT, len(STEPS))),
             pltpu.SemaphoreType.DMA((2 * NT, 2)),
             pltpu.SemaphoreType.DMA((2 * NT, 2)),
         ],

time: 60.8 us -> 57.8 us (0.951)
  Pallas kernels: 58.1 us -> 55.1 us
    pallas_call x1, Pallas kernels: 58.1 us -> 55.1 us  [per_device(): pl.pallas_call(block_kernel, out_shape=jax.ShapeDtypeStruct((TOK, C), BF)...]
where the time goes in v6:
time: 57.8 us; the launch traced here: 57.7 us
  Pallas kernels  55.1 us (95%)
  local copies, waits for them, and re-layouts  2.61 us (5%)
    pallas_call x1, Pallas kernels, per_device(): pl.pallas_call(block_kernel, out_shape=jax.ShapeDtypeStruct((TOK, C), BF)...  55.1 us
    unnamed x5, local copies, waits for them, and re-layouts  2.61 us

profile of v6, /device:TPU:17, one launch (start us, length us, event | category | flops | bytes accessed | tf_op | source)
XLA Modules:
  0.0 57.7 jit_solution(12859207861727149481)
XLA Ops:
  0.0 0.0 copy-start
  0.0 1.1 %copy-done = bf16[1,16,32,640]{3,2,1,0:T(8,128)(2,1)S(1)} copy-done((bf16[1,16,32,640]{3,2,1,0:T(8,128)(2,1)S(1)}, bf16[1,16,32,640]{3,2,1,0:T(8,128)(2,1)}, u32[]{:S(2)}) %copy-start) | copy-done | bytes 655384
  1.1 0.0 copy-start.1
  1.1 0.7 %copy-done.1 = bf16[640]{0:T(1024)(128)(2,1)S(1)} copy-done((bf16[640]{0:T(1024)(128)(2,1)S(1)}, bf16[640]{0:T(1024)(128)(2,1)}, u32[]{:S(2)}) %copy-start.1) | copy-done | bytes 1304
  1.8 55.1 %block.1 = bf16[512,640]{1,0:T(8,128)(2,1)S(1)} custom-call(bf16[512,640]{1,0:T(8,128)(2,1)S(1)} %bitcast.4, bf16[3,1920,640]{2,1,0:T(8,128)(2,1)} %bitcast.5, bf16[640]{0:T(1024)(128)(2,1)S(1)} %copy-done.1, bf16[640,640]{1,0:T(8,128)(2,1)} %wq_hbm.1, bf16[640,1280]{1,0:T(8,128)(2,1)} %wkv_hbm.1, bf16[640,640]{1,0:T(8,128)(2,1)} %wout_hbm.1), custom_call_target="tpu_custom_call" | custom-call | tf_op jit(solution)/shard_map/block/pallas_call | solution.py:353
  56.9 0.8 %copy.8 = bf16[1,16,32,640]{3,2,1,0:T(8,128)(2,1)} copy(bf16[1,16,32,640]{3,2,1,0:T(8,128)(2,1)S(1)} %bitcast.3) | data formatting | bytes 1310720
Async XLA Ops:
  0.0 1.1 %copy-start = (bf16[1,16,32,640]{3,2,1,0:T(8,128)(2,1)S(1)}, bf16[1,16,32,640]{3,2,1,0:T(8,128)(2,1)}, u32[]{:S(2)}) copy-start(bf16[1,16,32,640]{3,2,1,0:T(8,128)(2,1)} %param.6) | copy-start | bytes 1966084
  1.1 0.7 %copy-start.1 = (bf16[640]{0:T(1024)(128)(2,1)S(1)}, bf16[640]{0:T(1024)(128)(2,1)}, u32[]{:S(2)}) copy-start(bf16[640]{0:T(1024)(128)(2,1)} %b_ref.1) | copy-start | bytes 3844
